TPU v7x, 32 devices: a whole 2x2x4 slice. The times are simulated.
32 devices in a mesh: seq: 16 (over z, x, core), head: 2 (over y).
Axes of the slice: x: 2, y: 2, z: 4, core: 2. Of those that a mesh axis runs over, the one named last changes fastest.
Arguments:
- alignment_rows: bfloat16 [128, 1024, 256], P('seq'), may hold values from -16 to 16
- upstream_derivative_tensor: bfloat16 [128, 1024, 256], P(None, 'seq'), may hold values from -12 to 12
- saved_pair_bias: bfloat16 [8, 1024, 1024], P('head', 'seq'), may hold values from -360 to 360
- pairwise_features: bfloat16 [1024, 1024, 128], P('seq', 'head'), may hold values from -16 to 16
- sequence_layernorm_scaling: float32 [256], replicated, may hold values from 0.5 to 2
- sequence_layernorm_centre: float32 [256], replicated, may hold values from -1 to 1
- asking_projection_matrix: bfloat16 [256, 256], replicated, may hold values from -0.375 to 0.375
- matching_projection_matrix: bfloat16 [256, 256], replicated, may hold values from -0.375 to 0.375
- content_projection_matrix: bfloat16 [256, 256], replicated, may hold values from -0.375 to 0.375
- sigmoid_projection_matrix: bfloat16 [256, 256], replicated, may hold values from -0.375 to 0.375
- gate_offset_bias: float32 [256], replicated, may hold values from -2 to 2
- final_projection_matrix: bfloat16 [256, 256], replicated, may hold values from -0.375 to 0.375
- pairwise_norm_gain: float32 [128], replicated, may hold values from 0.5 to 2
- pairwise_weight: bfloat16 [128, 8], replicated, may hold values from -0.5 to 0.5
Outputs:
- alignment_input_gradient: bfloat16 [128, 1024, 256], P('seq', 'head')
- pairwise_gradient: bfloat16 [1024, 1024, 128], P('seq', 'head')
All inputs are finite; a program needn't handle non-finite values.
Results may differ from a plain program's by a relative error of at most 0.012.
The roundings to bfloat16 on the way count: a program that leaves them out, or rounds other values in their place, can miss the bound.
Values may be sent and summed in bfloat16 or wider, within the bound.
A program may use at most 320 MiB of HBM per device.

v0:
```python
import jax
import jax.numpy as jnp
from jax import lax
from jax.sharding import PartitionSpec as P

SUBSPACE_WIDTH = 32
epsilon = 1e-05


def layer_statistics(values):
    average = jnp.mean(values, axis=-1, keepdims=True)
    centred = values - average
    inverse_deviation = lax.rsqrt(jnp.mean(centred * centred, axis=-1, keepdims=True) + epsilon)
    return (centred * inverse_deviation, inverse_deviation)


def layer_reverse_step(upstream, standardized_values, inverse_deviation):
    first_mean = jnp.mean(upstream, axis=-1, keepdims=True)
    second_mean = jnp.mean(upstream * standardized_values, axis=-1, keepdims=True)
    return inverse_deviation * (upstream - first_mean - standardized_values * second_mean)


def per_device(
    alignment_rows,
    upstream_derivative_tensor,
    saved_pair_bias,
    pairwise_features,
    sequence_layernorm_scaling,
    sequence_layernorm_centre,
    asking_projection_matrix,
    matching_projection_matrix,
    content_projection_matrix,
    sigmoid_projection_matrix,
    gate_offset_bias,
    final_projection_matrix,
    pairwise_norm_gain,
    pairwise_weight,
):
    local_heads = saved_pair_bias.shape[0]
    all_heads = pairwise_weight.shape[1]
    resident_rows, residue_total, channel_count = alignment_rows.shape
    head_width = local_heads * SUBSPACE_WIDTH
    first_head = lax.axis_index("head") * local_heads
    first_col = first_head * SUBSPACE_WIDTH
    score_scale = SUBSPACE_WIDTH ** (-0.5)
    bias_full = lax.all_gather(saved_pair_bias, "seq", axis=1, tiled=True)
    standardized_values, inverse_deviation = layer_statistics(alignment_rows.astype(jnp.float32))
    normalized_rows = (
        standardized_values * sequence_layernorm_scaling + sequence_layernorm_centre
    ).astype(jnp.bfloat16)

    def project(coefficient_matrix):
        columns = lax.dynamic_slice_in_dim(coefficient_matrix, first_col, head_width, 1)
        return jnp.dot(normalized_rows, columns, preferred_element_type=jnp.float32)

    head_shape = (resident_rows, residue_total, local_heads, SUBSPACE_WIDTH)
    query = (
        (score_scale * project(asking_projection_matrix)).astype(jnp.bfloat16).reshape(head_shape)
    )
    keys_all = project(matching_projection_matrix).astype(jnp.bfloat16).reshape(head_shape)
    vals_all = project(content_projection_matrix).astype(jnp.bfloat16).reshape(head_shape)
    gate_shift = lax.dynamic_slice_in_dim(gate_offset_bias, first_col, head_width, 0)
    gate = jax.nn.sigmoid(project(sigmoid_projection_matrix) + gate_shift).reshape(head_shape)
    out_rows = lax.dynamic_slice_in_dim(final_projection_matrix, first_col, head_width, 0)
    row_grads = lax.all_to_all(
        upstream_derivative_tensor, "seq", split_axis=0, concat_axis=1, tiled=True
    )
    gated_grad = jnp.einsum(
        "src,wc->srw", row_grads, out_rows, preferred_element_type=jnp.float32
    ).astype(jnp.bfloat16)
    gated_grad = gated_grad.reshape(head_shape)
    bias_float = bias_full.astype(jnp.float32)

    def row_reverse_step(pair_bias_gradient, layer_inputs):
        query_row, keys_row, vals_row, gate_row, row_gradient = layer_inputs
        logits = (
            jnp.einsum("ihd,jhd->hij", query_row, keys_row, preferred_element_type=jnp.float32)
            + bias_float
        )
        probs = jax.nn.softmax(logits, axis=-1)
        probs_low = probs.astype(jnp.bfloat16)
        attended = jnp.einsum(
            "hij,jhd->ihd", probs_low, vals_row, preferred_element_type=jnp.float32
        )
        grad_float = row_gradient.astype(jnp.float32)
        attended_grad = (grad_float * gate_row).astype(jnp.bfloat16)
        gate_grad = (grad_float * attended * gate_row * (1.0 - gate_row)).astype(jnp.bfloat16)
        prob_grad = jnp.einsum(
            "ihd,jhd->hij", attended_grad, vals_row, preferred_element_type=jnp.float32
        )
        inner_sum = jnp.sum(probs * prob_grad, axis=-1, keepdims=True)
        score_grad = probs * (prob_grad - inner_sum)
        score_low = score_grad.astype(jnp.bfloat16)
        query_grad = (
            score_scale
            * jnp.einsum("hij,jhd->ihd", score_low, keys_row, preferred_element_type=jnp.float32)
        ).astype(jnp.bfloat16)
        key_grad = jnp.einsum(
            "hij,ihd->jhd", score_low, query_row, preferred_element_type=jnp.float32
        ).astype(jnp.bfloat16)
        value_grad = jnp.einsum(
            "hij,ihd->jhd", probs_low, attended_grad, preferred_element_type=jnp.float32
        ).astype(jnp.bfloat16)
        grads = jnp.concatenate([query_grad, key_grad, value_grad, gate_grad], axis=-1)
        return (pair_bias_gradient + score_grad, grads)

    pair_bias_gradient, head_grad_rows = lax.scan(
        row_reverse_step,
        jnp.zeros((local_heads, residue_total, residue_total), jnp.float32),
        (query, keys_all, vals_all, gate, gated_grad),
    )
    piled_arrays = jnp.stack(
        [
            coefficient_matrix.reshape(channel_count, all_heads, SUBSPACE_WIDTH)
            for coefficient_matrix in (
                asking_projection_matrix,
                matching_projection_matrix,
                content_projection_matrix,
                sigmoid_projection_matrix,
            )
        ],
        axis=2,
    )
    piled_arrays = piled_arrays.reshape(channel_count, all_heads, 4 * SUBSPACE_WIDTH)
    local_weight = lax.dynamic_slice_in_dim(piled_arrays, first_head, local_heads, 1)
    partial_term = jnp.einsum(
        "srhf,chf->src", head_grad_rows, local_weight, preferred_element_type=jnp.float32
    )
    normalized_gradient = lax.psum_scatter(
        partial_term.astype(jnp.bfloat16), "head", scatter_dimension=1, tiled=True
    ).astype(jnp.float32)
    block_len = residue_total // lax.axis_size("head")
    block_start = lax.axis_index("head") * block_len
    normalized_block = lax.dynamic_slice_in_dim(standardized_values, block_start, block_len, 1)
    inverse_spread_block = lax.dynamic_slice_in_dim(inverse_deviation, block_start, block_len, 1)
    alignment_input_gradient = layer_reverse_step(
        normalized_gradient * sequence_layernorm_scaling, normalized_block, inverse_spread_block
    ).astype(jnp.bfloat16)
    summed_rows = lax.psum_scatter(pair_bias_gradient, "seq", scatter_dimension=1, tiled=True)
    bias_tile = lax.all_to_all(
        summed_rows.astype(jnp.bfloat16), "head", split_axis=2, concat_axis=0, tiled=True
    ).astype(summed_rows.dtype)
    bias_low = bias_tile.astype(jnp.bfloat16)
    pair_hat, pair_inv = layer_statistics(pairwise_features.astype(jnp.float32))
    pair_normed_grad = jnp.einsum(
        "hij,ch->ijc", bias_low, pairwise_weight, preferred_element_type=jnp.float32
    )
    pairwise_gradient = layer_reverse_step(
        pair_normed_grad * pairwise_norm_gain, pair_hat, pair_inv
    ).astype(jnp.bfloat16)
    return (alignment_input_gradient, pairwise_gradient)


def solution(mesh):
    placed = (
        P("seq", None, None),
        P(None, "seq", None),
        P("head", "seq", None),
        P("seq", "head", None),
        P(),
        P(),
        P(),
        P(),
        P(),
        P(),
        P(),
        P(),
        P(),
        P(),
    )
    return jax.shard_map(
        per_device,
        mesh=mesh,
        in_specs=placed,
        out_specs=(P("seq", "head", None), P("seq", "head", None)),
        check_vma=False,
    )
```

profile of v0, /device:TPU:10, one launch (start us, length us, event | category | flops | bytes accessed | tf_op | source)
XLA Modules:
  0.0 1453.9 jit_solution(13815604666751804673)
XLA Ops:
  9.7 6.3 all-to-all-start
  16.5 12.0 copy.72
  34.3 4.8 fusion.63
  48.7 5.2 fusion.61
  61.9 5.0 add_divide_fusion
  66.9 91.8 %all-to-all-done = bf16[128,64,256]{2,1,0:T(8,128)(2,1)} async-done(((bf16[128,64,256]{2,1,0:T(8,128)(2,1)}), bf16[128,64,256]{2,1,0:T(8,128)(2,1)}, u32[]{:S(2)}, u32[]{:S(2)}) %all-to-all-start) | async-done | bytes 4194336 | tf_op jit(solution)/shard_map/all_to_all | solution.py:65
  164.0 15.8 %copy.64 = f32[4,1024,1024]{1,2,0:T(8,128)} copy(bf16[4,1024,1024]{2,0,1:T(4,128)(2,1)} %all-gather.2.cloned.1.call-done) | data formatting | bytes 25165824
  179.9 820.5 %while.13 = (s32[]{:T(128)}, f32[4,1024,1024]{1,2,0:T(8,128)}, bf16[8,1024,4,128]{1,3,2,0:T(8,128)(2,1)}, bf16[8,1024,4,32]{1,3,2,0:T(8,128)(2,1)}, bf16[8,1024,...) while((s32[]{:T(128)}, f32[4,1024,1024]{1,2,0:T(8,128)}, ...), condition=%wide.region_6.7_spmd.clone, body=%wide.region_2.6_spmd.clone.sunk | while | flops 1692408832 | bytes 267244176 | solution.py:107
  189.9 13.9 convolution_add_fusion.2
  203.9 18.6 %fusion.127 = (f32[4,1024]{1,0:T(4,128)S(1)}, f32[4,1024,1024]{1,2,0:T(8,128)}) fusion(f32[4,1024,1024]{1,2,0:T(8,128)} %convolution_add_fusion.2), kind=kOutput, calls=%fused_computation.106.clone.1 | output fusion | flops 8389631 | bytes 33570816 | tf_op jit(solution)/shard_map/while/body/eval_jaxpr/sub | solution.py:80
  222.5 14.3 multiply_reduce_fusion.4
  236.8 17.3 %fusion.128 = (bf16[4,1024,1024]{1,2,0:T(8,128)(2,1)S(1)}, f32[4,1024,1024]{1,2,0:T(8,128)}) fusion(f32[4,1024,1024]{1,2,0:T(8,128)} %get-tuple-element.193, f32[4,1024]{1,0:T(4,128)S(1)} %get-tuple-element.194, f32[4,1024,1024]{1,2,0:T(8,128)} %get-tuple-element.191, f32[4,1024]{1,0:T(4,128)S(1)} %get-tuple-element.192, ...), kind=kLoop, calls=%fused_computation.7.clone.1 | loop fusion | flops 25165824 | bytes 75530240 | tf_op jit(solution)/shard_map/while/body/eval_jaxpr/convert_element_type | solution.py:93
  259.1 12.8 fusion.129
  272.0 12.9 fusion.130
  286.0 13.9 convolution_add_fusion.2
  299.9 18.6 %fusion.127 = (f32[4,1024]{1,0:T(4,128)S(1)}, f32[4,1024,1024]{1,2,0:T(8,128)}) fusion(f32[4,1024,1024]{1,2,0:T(8,128)} %convolution_add_fusion.2), kind=kOutput, calls=%fused_computation.106.clone.1 | output fusion | flops 8389631 | bytes 33570816 | tf_op jit(solution)/shard_map/while/body/eval_jaxpr/sub | solution.py:80
  318.5 14.3 multiply_reduce_fusion.4
  332.8 23.3 %fusion.128 = (bf16[4,1024,1024]{1,2,0:T(8,128)(2,1)S(1)}, f32[4,1024,1024]{1,2,0:T(8,128)}) fusion(f32[4,1024,1024]{1,2,0:T(8,128)} %get-tuple-element.193, f32[4,1024]{1,0:T(4,128)S(1)} %get-tuple-element.194, f32[4,1024,1024]{1,2,0:T(8,128)} %get-tuple-element.191, f32[4,1024]{1,0:T(4,128)S(1)} %get-tuple-element.192, ...), kind=kLoop, calls=%fused_computation.7.clone.1 | loop fusion | flops 25165824 | bytes 75530240 | tf_op jit(solution)/shard_map/while/body/eval_jaxpr/convert_element_type | solution.py:93
  361.2 12.8 fusion.129
  374.0 12.9 fusion.130
  388.0 13.9 convolution_add_fusion.2
  402.0 18.6 %fusion.127 = (f32[4,1024]{1,0:T(4,128)S(1)}, f32[4,1024,1024]{1,2,0:T(8,128)}) fusion(f32[4,1024,1024]{1,2,0:T(8,128)} %convolution_add_fusion.2), kind=kOutput, calls=%fused_computation.106.clone.1 | output fusion | flops 8389631 | bytes 33570816 | tf_op jit(solution)/shard_map/while/body/eval_jaxpr/sub | solution.py:80
  420.6 14.3 multiply_reduce_fusion.4
  434.9 23.3 %fusion.128 = (bf16[4,1024,1024]{1,2,0:T(8,128)(2,1)S(1)}, f32[4,1024,1024]{1,2,0:T(8,128)}) fusion(f32[4,1024,1024]{1,2,0:T(8,128)} %get-tuple-element.193, f32[4,1024]{1,0:T(4,128)S(1)} %get-tuple-element.194, f32[4,1024,1024]{1,2,0:T(8,128)} %get-tuple-element.191, f32[4,1024]{1,0:T(4,128)S(1)} %get-tuple-element.192, ...), kind=kLoop, calls=%fused_computation.7.clone.1 | loop fusion | flops 25165824 | bytes 75530240 | tf_op jit(solution)/shard_map/while/body/eval_jaxpr/convert_element_type | solution.py:93
  463.2 12.8 fusion.129
  476.1 12.9 fusion.130
  490.1 13.9 convolution_add_fusion.2
  504.0 18.6 %fusion.127 = (f32[4,1024]{1,0:T(4,128)S(1)}, f32[4,1024,1024]{1,2,0:T(8,128)}) fusion(f32[4,1024,1024]{1,2,0:T(8,128)} %convolution_add_fusion.2), kind=kOutput, calls=%fused_computation.106.clone.1 | output fusion | flops 8389631 | bytes 33570816 | tf_op jit(solution)/shard_map/while/body/eval_jaxpr/sub | solution.py:80
  522.6 14.3 multiply_reduce_fusion.4
  536.9 23.3 %fusion.128 = (bf16[4,1024,1024]{1,2,0:T(8,128)(2,1)S(1)}, f32[4,1024,1024]{1,2,0:T(8,128)}) fusion(f32[4,1024,1024]{1,2,0:T(8,128)} %get-tuple-element.193, f32[4,1024]{1,0:T(4,128)S(1)} %get-tuple-element.194, f32[4,1024,1024]{1,2,0:T(8,128)} %get-tuple-element.191, f32[4,1024]{1,0:T(4,128)S(1)} %get-tuple-element.192, ...), kind=kLoop, calls=%fused_computation.7.clone.1 | loop fusion | flops 25165824 | bytes 75530240 | tf_op jit(solution)/shard_map/while/body/eval_jaxpr/convert_element_type | solution.py:93
  565.3 12.9 fusion.129
  578.2 12.9 fusion.130
  592.2 13.9 convolution_add_fusion.2
  606.1 18.6 %fusion.127 = (f32[4,1024]{1,0:T(4,128)S(1)}, f32[4,1024,1024]{1,2,0:T(8,128)}) fusion(f32[4,1024,1024]{1,2,0:T(8,128)} %convolution_add_fusion.2), kind=kOutput, calls=%fused_computation.106.clone.1 | output fusion | flops 8389631 | bytes 33570816 | tf_op jit(solution)/shard_map/while/body/eval_jaxpr/sub | solution.py:80
  624.7 14.3 multiply_reduce_fusion.4
  639.0 23.3 %fusion.128 = (bf16[4,1024,1024]{1,2,0:T(8,128)(2,1)S(1)}, f32[4,1024,1024]{1,2,0:T(8,128)}) fusion(f32[4,1024,1024]{1,2,0:T(8,128)} %get-tuple-element.193, f32[4,1024]{1,0:T(4,128)S(1)} %get-tuple-element.194, f32[4,1024,1024]{1,2,0:T(8,128)} %get-tuple-element.191, f32[4,1024]{1,0:T(4,128)S(1)} %get-tuple-element.192, ...), kind=kLoop, calls=%fused_computation.7.clone.1 | loop fusion | flops 25165824 | bytes 75530240 | tf_op jit(solution)/shard_map/while/body/eval_jaxpr/convert_element_type | solution.py:93
  667.4 12.8 fusion.129
  680.2 12.9 fusion.130
  694.2 13.9 convolution_add_fusion.2
  708.1 18.6 %fusion.127 = (f32[4,1024]{1,0:T(4,128)S(1)}, f32[4,1024,1024]{1,2,0:T(8,128)}) fusion(f32[4,1024,1024]{1,2,0:T(8,128)} %convolution_add_fusion.2), kind=kOutput, calls=%fused_computation.106.clone.1 | output fusion | flops 8389631 | bytes 33570816 | tf_op jit(solution)/shard_map/while/body/eval_jaxpr/sub | solution.py:80
  726.7 14.3 multiply_reduce_fusion.4
  741.0 23.3 %fusion.128 = (bf16[4,1024,1024]{1,2,0:T(8,128)(2,1)S(1)}, f32[4,1024,1024]{1,2,0:T(8,128)}) fusion(f32[4,1024,1024]{1,2,0:T(8,128)} %get-tuple-element.193, f32[4,1024]{1,0:T(4,128)S(1)} %get-tuple-element.194, f32[4,1024,1024]{1,2,0:T(8,128)} %get-tuple-element.191, f32[4,1024]{1,0:T(4,128)S(1)} %get-tuple-element.192, ...), kind=kLoop, calls=%fused_computation.7.clone.1 | loop fusion | flops 25165824 | bytes 75530240 | tf_op jit(solution)/shard_map/while/body/eval_jaxpr/convert_element_type | solution.py:93
  769.4 12.8 fusion.129
  782.2 12.9 fusion.130
  796.2 13.9 convolution_add_fusion.2
  810.2 18.6 %fusion.127 = (f32[4,1024]{1,0:T(4,128)S(1)}, f32[4,1024,1024]{1,2,0:T(8,128)}) fusion(f32[4,1024,1024]{1,2,0:T(8,128)} %convolution_add_fusion.2), kind=kOutput, calls=%fused_computation.106.clone.1 | output fusion | flops 8389631 | bytes 33570816 | tf_op jit(solution)/shard_map/while/body/eval_jaxpr/sub | solution.py:80
  828.8 14.3 multiply_reduce_fusion.4
  843.1 23.3 %fusion.128 = (bf16[4,1024,1024]{1,2,0:T(8,128)(2,1)S(1)}, f32[4,1024,1024]{1,2,0:T(8,128)}) fusion(f32[4,1024,1024]{1,2,0:T(8,128)} %get-tuple-element.193, f32[4,1024]{1,0:T(4,128)S(1)} %get-tuple-element.194, f32[4,1024,1024]{1,2,0:T(8,128)} %get-tuple-element.191, f32[4,1024]{1,0:T(4,128)S(1)} %get-tuple-element.192, ...), kind=kLoop, calls=%fused_computation.7.clone.1 | loop fusion | flops 25165824 | bytes 75530240 | tf_op jit(solution)/shard_map/while/body/eval_jaxpr/convert_element_type | solution.py:93
  871.5 12.8 fusion.129
  884.3 12.9 fusion.130
  898.3 13.9 convolution_add_fusion.2
  912.2 18.6 %fusion.127 = (f32[4,1024]{1,0:T(4,128)S(1)}, f32[4,1024,1024]{1,2,0:T(8,128)}) fusion(f32[4,1024,1024]{1,2,0:T(8,128)} %convolution_add_fusion.2), kind=kOutput, calls=%fused_computation.106.clone.1 | output fusion | flops 8389631 | bytes 33570816 | tf_op jit(solution)/shard_map/while/body/eval_jaxpr/sub | solution.py:80
  930.8 14.3 multiply_reduce_fusion.4
  945.1 23.3 %fusion.128 = (bf16[4,1024,1024]{1,2,0:T(8,128)(2,1)S(1)}, f32[4,1024,1024]{1,2,0:T(8,128)}) fusion(f32[4,1024,1024]{1,2,0:T(8,128)} %get-tuple-element.193, f32[4,1024]{1,0:T(4,128)S(1)} %get-tuple-element.194, f32[4,1024,1024]{1,2,0:T(8,128)} %get-tuple-element.191, f32[4,1024]{1,0:T(4,128)S(1)} %get-tuple-element.192, ...), kind=kLoop, calls=%fused_computation.7.clone.1 | loop fusion | flops 25165824 | bytes 75530240 | tf_op jit(solution)/shard_map/while/body/eval_jaxpr/convert_element_type | solution.py:93
  973.5 12.8 fusion.129
  986.3 12.9 fusion.130
  1000.3 20.2 %copy.73 = f32[4,1024,1024]{2,0,1:T(4,128)} copy(f32[4,1024,1024]{1,2,0:T(8,128)} %get-tuple-element.51) | data formatting | bytes 33554432 | tf_op jit(solution)/shard_map/while | solution.py:107
  1020.6 7.7 bitcast_convert_fusion
  1028.3 364.2 %all-reduce.2 = bf16[4,1024,1024]{2,0,1:T(4,128)(2,1)} all-reduce(f32[4,1024,1024]{2,0,1:T(4,128)} %copy.73), channel_id=3, replica_groups=mesh['seq'=16,'head'=2] {'seq'}, use_global_device_ids=true, to_apply=%region_12.13.clone | all-reduce | flops 4194304 | bytes 25165824
  1399.8 6.5 all-to-all-done.1
  1407.9 7.7 multiply_reduce_fusion.1
  1415.7 9.5 fusion.59
  1425.2 12.0 copy.76
  1441.2 5.5 multiply_convert_fusion
  (106 shorter events, 92.7 us)
Async XLA Ops:
  7.2 154.0 %copy-start = (bf16[256,256]{1,0:T(8,128)(2,1)S(1)}, bf16[256,256]{1,0:T(8,128)(2,1)}, u32[]{:S(2)}) copy-start(bf16[256,256]{1,0:T(8,128)(2,1)} %param.27) | copy-start | bytes 393220
  7.2 8.8 copy-start.10
  7.2 8.9 copy-start.11
  7.2 9.0 copy-start.12
  7.2 9.1 copy-start.13
  7.2 156.8 %all-gather.2.cloned.1.call-start = ((), (), s32[]{:S(2)}) async-start(), calls=%async_computation.3 | async-start | bytes 8912896 | tf_op jit(solution)/shard_map/all_gather | solution.py:46
  9.7 149.0 %all-to-all-start = ((bf16[128,64,256]{2,1,0:T(8,128)(2,1)}), bf16[128,64,256]{2,1,0:T(8,128)(2,1)}, u32[]{:S(2)}, u32[]{:S(2)}) async-start(bf16[128,64,256]{2,1,0:T(8,128)(2,1)} %param.17), calls=%async_computation | async-start | bytes 8388608 | tf_op jit(solution)/shard_map/all_to_all | solution.py:65
  15.9 1421.3 %reduce-scatter.2.cloned.1.call-start = ((), (), s32[]{:S(2)}) async-start(), calls=%async_computation.4 | async-start | bytes 6291456 | tf_op jit(solution)/shard_map/reduce_scatter | solution.py:129
  16.5 12.9 copy-start.18
  16.5 13.0 copy-start.20
  30.7 8.4 copy-start.2
  30.7 10.5 copy-start.3
  30.7 10.5 copy-start.14
  30.7 10.5 copy-start.19
  39.1 22.8 %copy-start.8 = (f32[8,1024]{1,0:T(8,128)}, f32[8,1024]{1,0:T(8,128)S(1)}, u32[]{:S(2)}) copy-start(f32[8,1024]{1,0:T(8,128)S(1)} %add_rsqrt_fusion.1) | copy-start | bytes 98308
  41.2 16.8 %copy-start.4 = (f32[64,512]{1,0:T(8,128)}, f32[64,512]{1,0:T(8,128)S(1)}, u32[]{:S(2)}) copy-start(f32[64,512]{1,0:T(8,128)S(1)} %broadcast_multiply_fusion.2) | copy-start | bytes 393220
  1000.3 20.2 %copy-start.7 = (bf16[256,8,4,32]{0,3,2,1:T(8,128)(2,1)S(1)}, bf16[256,8,4,32]{0,3,2,1:T(8,128)(2,1)}, u32[]{:S(2)}) copy-start(bf16[256,8,4,32]{0,3,2,1:T(8,128)(2,1)} %copy.69) | copy-start | bytes 1572868
  1028.3 371.4 %copy-start.9 = (f32[8,1024]{1,0:T(8,128)S(1)}, f32[8,1024]{1,0:T(8,128)}, u32[]{:S(2)}) copy-start(f32[8,1024]{1,0:T(8,128)} %copy-done.8) | copy-start | bytes 98308
  1028.3 371.4 %copy-start.6 = (f32[64,512]{1,0:T(8,128)S(1)}, f32[64,512]{1,0:T(8,128)}, u32[]{:S(2)}) copy-start(f32[64,512]{1,0:T(8,128)} %fusion.60) | copy-start | bytes 393220
  1392.5 15.4 %copy-start.5 = (f32[64,512]{1,0:T(8,128)S(1)}, f32[64,512]{1,0:T(8,128)}, u32[]{:S(2)}) copy-start(f32[64,512]{1,0:T(8,128)} %copy-done.4) | copy-start | bytes 393220
  1392.5 15.4 %copy-start.16 = (f32[128]{0:T(128)S(1)}, f32[128]{0:T(128)}, u32[]{:S(2)}) copy-start(f32[128]{0:T(128)} %param.28) | copy-start | bytes 1540
  1392.5 15.4 %copy-start.17 = (bf16[128,8]{0,1:T(8,128)(2,1)S(1)}, bf16[128,8]{0,1:T(8,128)(2,1)}, u32[]{:S(2)}) copy-start(bf16[128,8]{0,1:T(8,128)(2,1)} %param.29) | copy-start | bytes 6148
  1396.2 10.1 all-to-all-start.1
  1425.2 12.0 copy-start.15
  1425.2 21.5 %copy-start.1 = (bf16[256,256]{1,0:T(8,128)(2,1)S(1)}, bf16[256,256]{1,0:T(8,128)(2,1)}, u32[]{:S(2)}) copy-start(bf16[256,256]{1,0:T(8,128)(2,1)} %param.27) | copy-start | bytes 393220
Sparse Core Ops, SparseCore 0:
  10.2 136.0 all-gather.1
  1028.4 54.2 reduce-scatter.1
where the time goes:
time: 1470 us; the launch traced here: 1450 us
  matrix products  507 us (34%)
  other arithmetic  376 us (26%)
  blocking collectives  364 us (25%)
  waiting for transfers between devices  98.3 us (7%)
  local copies, waits for them, and re-layouts  72.1 us (5%)
  between operations  15.5 us (1%)
    unnamed x1, blocking collectives  364 us
    convert_element_type x8, other arithmetic, row_reverse_step(): score_low = score_grad.astype(jnp.bfloat16)  180 us
    sub x8, other arithmetic, row_reverse_step(): probs = jax.nn.softmax(logits, axis=-1)  149 us
    dot_general x8, matrix products, row_reverse_step(): jnp.einsum('ihd,jhd->hij', attended_grad, vals_row, preferred_element_typ...  114 us
    dot_general x8, matrix products, row_reverse_step(): jnp.einsum('ihd,jhd->hij', query_row, keys_row, preferred_element_type=jn...  112 us
    dot_general x8, matrix products, row_reverse_step(): jnp.einsum('hij,ihd->jhd', probs_low, attended_grad, preferred_element_ty...  104 us
    dot_general x8, matrix products, row_reverse_step(): jnp.einsum('hij,jhd->ihd', probs_low, vals_row, preferred_element_type=jn...  103 us
    all_to_all x1, waiting for transfers between devices, per_device(): lax.all_to_all(upstream_derivative_tensor, 'seq', split_axis=0, concat_ax...  91.8 us
  transfers between devices with their start and end apart: 4, of which 2 were waited for; matrix products, arithmetic and copies ran while one was open for 6% of the time, Pallas kernels for 0%

commit v1 on v0

--- a/solution.py
+++ b/solution.py
@@ -62,8 +62,16 @@
     gate_shift = lax.dynamic_slice_in_dim(gate_offset_bias, first_col, head_width, 0)
     gate = jax.nn.sigmoid(project(sigmoid_projection_matrix) + gate_shift).reshape(head_shape)
     out_rows = lax.dynamic_slice_in_dim(final_projection_matrix, first_col, head_width, 0)
-    row_grads = lax.all_to_all(
-        upstream_derivative_tensor, "seq", split_axis=0, concat_axis=1, tiled=True
+    row_grads = jnp.concatenate(
+        jax.lax.all_to_all(
+            jnp.stack(
+                jnp.split(upstream_derivative_tensor, jax.lax.axis_size("seq"), axis=0), axis=0
+            ),
+            concat_axis=0,
+            split_axis=0,
+            axis_name="seq",
+        ),
+        axis=1,
     )
     gated_grad = jnp.einsum(
         "src,wc->srw", row_grads, out_rows, preferred_element_type=jnp.float32

time: 1470 us -> 1480 us (level)
  local copies, waits for them, and re-layouts: 72.1 us -> 98.3 us
  waiting for transfers between devices: 98.3 us -> 82.1 us
    unnamed x53 -> x68, local copies, waits for them, and re-layouts: 45.5 us -> 69.9 us
    all_to_all x1, waiting for transfers between devices: 91.8 us -> 75.6 us  [per_device(): jax.lax.all_to_all(jnp.stack(jnp.split(upstream_derivative_tensor, jax.la...]
  transfers between devices with their start and end apart: 4 -> 4, of which waited for: 2 -> 2; matrix products, arithmetic and copies ran while one was open for 6% -> 8% of each run, Pallas kernels for 0% -> 0%
where the time goes in v1:
time: 1480 us; the launch traced here: 1460 us
  matrix products  507 us (34%)
  other arithmetic  376 us (25%)
  blocking collectives  364 us (25%)
  local copies, waits for them, and re-layouts  98.3 us (7%)
  waiting for transfers between devices  82.1 us (6%)
  between operations  15.5 us (1%)
    unnamed x1, blocking collectives  364 us
    convert_element_type x8, other arithmetic, row_reverse_step(): score_low = score_grad.astype(jnp.bfloat16)  180 us
    sub x8, other arithmetic, row_reverse_step(): probs = jax.nn.softmax(logits, axis=-1)  149 us
    dot_general x8, matrix products, row_reverse_step(): jnp.einsum('ihd,jhd->hij', attended_grad, vals_row, preferred_element_typ...  114 us
    dot_general x8, matrix products, row_reverse_step(): jnp.einsum('ihd,jhd->hij', query_row, keys_row, preferred_element_type=jn...  112 us
    dot_general x8, matrix products, row_reverse_step(): jnp.einsum('hij,ihd->jhd', probs_low, attended_grad, preferred_element_ty...  104 us
    dot_general x8, matrix products, row_reverse_step(): jnp.einsum('hij,jhd->ihd', probs_low, vals_row, preferred_element_type=jn...  103 us
    all_to_all x1, waiting for transfers between devices, per_device(): jax.lax.all_to_all(jnp.stack(jnp.split(upstream_derivative_tensor, jax.la...  75.6 us
  transfers between devices with their start and end apart: 4, of which 2 were waited for; matrix products, arithmetic and copies ran while one was open for 8% of the time, Pallas kernels for 0%

profile of v1, /device:TPU:10, one launch (start us, length us, event | category | flops | bytes accessed | tf_op | source)
XLA Modules:
  0.0 1463.9 jit_solution(17102461964424623337)
XLA Ops:
  36.5 6.2 all-to-all-start
  43.3 11.2 copy.72
  60.4 4.9 fusion.63
  74.9 5.2 fusion.61
  88.0 5.0 add_divide_fusion
  93.0 75.6 %all-to-all-done = bf16[16,8,64,256]{3,2,1,0:T(8,128)(2,1)} async-done(((bf16[16,8,64,256]{3,2,1,0:T(8,128)(2,1)}), bf16[16,8,64,256]{3,2,1,0:T(8,128)(2,1)}, u32[]{:S(2)}, u32[]{:S(2)}) %all-to-all-start) | async-done | bytes 4194336 | tf_op jit(solution)/shard_map/all_to_all | solution.py:66
  174.0 15.8 %copy.64 = f32[4,1024,1024]{1,2,0:T(8,128)} copy(bf16[4,1024,1024]{2,0,1:T(4,128)(2,1)} %all-gather.2.cloned.1.call-done) | data formatting | bytes 25165824
  189.8 820.5 %while.13 = (s32[]{:T(128)}, f32[4,1024,1024]{1,2,0:T(8,128)}, bf16[8,1024,4,128]{1,3,2,0:T(8,128)(2,1)}, bf16[8,1024,4,32]{1,3,2,0:T(8,128)(2,1)}, bf16[8,1024,...) while((s32[]{:T(128)}, f32[4,1024,1024]{1,2,0:T(8,128)}, ...), condition=%wide.region_6.7_spmd.clone, body=%wide.region_2.6_spmd.clone.sunk | while | flops 1692408832 | bytes 267244176 | solution.py:115
  199.8 13.9 convolution_add_fusion.2
  213.8 18.6 %fusion.127 = (f32[4,1024]{1,0:T(4,128)S(1)}, f32[4,1024,1024]{1,2,0:T(8,128)}) fusion(f32[4,1024,1024]{1,2,0:T(8,128)} %convolution_add_fusion.2), kind=kOutput, calls=%fused_computation.122.clone.1 | output fusion | flops 8389631 | bytes 33570816 | tf_op jit(solution)/shard_map/while/body/eval_jaxpr/sub | solution.py:88
  232.4 14.3 multiply_reduce_fusion.4
  246.7 17.3 %fusion.128 = (bf16[4,1024,1024]{1,2,0:T(8,128)(2,1)S(1)}, f32[4,1024,1024]{1,2,0:T(8,128)}) fusion(f32[4,1024,1024]{1,2,0:T(8,128)} %get-tuple-element.193, f32[4,1024]{1,0:T(4,128)S(1)} %get-tuple-element.194, f32[4,1024,1024]{1,2,0:T(8,128)} %get-tuple-element.191, f32[4,1024]{1,0:T(4,128)S(1)} %get-tuple-element.192, ...), kind=kLoop, calls=%fused_computation.7.clone.1 | loop fusion | flops 25165824 | bytes 75530240 | tf_op jit(solution)/shard_map/while/body/eval_jaxpr/convert_element_type | solution.py:101
  269.1 12.8 fusion.129
  281.9 12.9 fusion.130
  295.9 13.9 convolution_add_fusion.2
  309.8 18.6 %fusion.127 = (f32[4,1024]{1,0:T(4,128)S(1)}, f32[4,1024,1024]{1,2,0:T(8,128)}) fusion(f32[4,1024,1024]{1,2,0:T(8,128)} %convolution_add_fusion.2), kind=kOutput, calls=%fused_computation.122.clone.1 | output fusion | flops 8389631 | bytes 33570816 | tf_op jit(solution)/shard_map/while/body/eval_jaxpr/sub | solution.py:88
  328.4 14.3 multiply_reduce_fusion.4
  342.7 23.3 %fusion.128 = (bf16[4,1024,1024]{1,2,0:T(8,128)(2,1)S(1)}, f32[4,1024,1024]{1,2,0:T(8,128)}) fusion(f32[4,1024,1024]{1,2,0:T(8,128)} %get-tuple-element.193, f32[4,1024]{1,0:T(4,128)S(1)} %get-tuple-element.194, f32[4,1024,1024]{1,2,0:T(8,128)} %get-tuple-element.191, f32[4,1024]{1,0:T(4,128)S(1)} %get-tuple-element.192, ...), kind=kLoop, calls=%fused_computation.7.clone.1 | loop fusion | flops 25165824 | bytes 75530240 | tf_op jit(solution)/shard_map/while/body/eval_jaxpr/convert_element_type | solution.py:101
  371.1 12.8 fusion.129
  383.9 12.9 fusion.130
  397.9 13.9 convolution_add_fusion.2
  411.9 18.6 %fusion.127 = (f32[4,1024]{1,0:T(4,128)S(1)}, f32[4,1024,1024]{1,2,0:T(8,128)}) fusion(f32[4,1024,1024]{1,2,0:T(8,128)} %convolution_add_fusion.2), kind=kOutput, calls=%fused_computation.122.clone.1 | output fusion | flops 8389631 | bytes 33570816 | tf_op jit(solution)/shard_map/while/body/eval_jaxpr/sub | solution.py:88
  430.5 14.3 multiply_reduce_fusion.4
  444.8 23.3 %fusion.128 = (bf16[4,1024,1024]{1,2,0:T(8,128)(2,1)S(1)}, f32[4,1024,1024]{1,2,0:T(8,128)}) fusion(f32[4,1024,1024]{1,2,0:T(8,128)} %get-tuple-element.193, f32[4,1024]{1,0:T(4,128)S(1)} %get-tuple-element.194, f32[4,1024,1024]{1,2,0:T(8,128)} %get-tuple-element.191, f32[4,1024]{1,0:T(4,128)S(1)} %get-tuple-element.192, ...), kind=kLoop, calls=%fused_computation.7.clone.1 | loop fusion | flops 25165824 | bytes 75530240 | tf_op jit(solution)/shard_map/while/body/eval_jaxpr/convert_element_type | solution.py:101
  473.2 12.8 fusion.129
  486.0 12.9 fusion.130
  500.0 13.9 convolution_add_fusion.2
  513.9 18.6 %fusion.127 = (f32[4,1024]{1,0:T(4,128)S(1)}, f32[4,1024,1024]{1,2,0:T(8,128)}) fusion(f32[4,1024,1024]{1,2,0:T(8,128)} %convolution_add_fusion.2), kind=kOutput, calls=%fused_computation.122.clone.1 | output fusion | flops 8389631 | bytes 33570816 | tf_op jit(solution)/shard_map/while/body/eval_jaxpr/sub | solution.py:88
  532.5 14.3 multiply_reduce_fusion.4
  546.8 23.3 %fusion.128 = (bf16[4,1024,1024]{1,2,0:T(8,128)(2,1)S(1)}, f32[4,1024,1024]{1,2,0:T(8,128)}) fusion(f32[4,1024,1024]{1,2,0:T(8,128)} %get-tuple-element.193, f32[4,1024]{1,0:T(4,128)S(1)} %get-tuple-element.194, f32[4,1024,1024]{1,2,0:T(8,128)} %get-tuple-element.191, f32[4,1024]{1,0:T(4,128)S(1)} %get-tuple-element.192, ...), kind=kLoop, calls=%fused_computation.7.clone.1 | loop fusion | flops 25165824 | bytes 75530240 | tf_op jit(solution)/shard_map/while/body/eval_jaxpr/convert_element_type | solution.py:101
  575.2 12.9 fusion.129
  588.1 12.9 fusion.130
  602.1 13.9 convolution_add_fusion.2
  616.0 18.6 %fusion.127 = (f32[4,1024]{1,0:T(4,128)S(1)}, f32[4,1024,1024]{1,2,0:T(8,128)}) fusion(f32[4,1024,1024]{1,2,0:T(8,128)} %convolution_add_fusion.2), kind=kOutput, calls=%fused_computation.122.clone.1 | output fusion | flops 8389631 | bytes 33570816 | tf_op jit(solution)/shard_map/while/body/eval_jaxpr/sub | solution.py:88
  634.6 14.3 multiply_reduce_fusion.4
  648.9 23.3 %fusion.128 = (bf16[4,1024,1024]{1,2,0:T(8,128)(2,1)S(1)}, f32[4,1024,1024]{1,2,0:T(8,128)}) fusion(f32[4,1024,1024]{1,2,0:T(8,128)} %get-tuple-element.193, f32[4,1024]{1,0:T(4,128)S(1)} %get-tuple-element.194, f32[4,1024,1024]{1,2,0:T(8,128)} %get-tuple-element.191, f32[4,1024]{1,0:T(4,128)S(1)} %get-tuple-element.192, ...), kind=kLoop, calls=%fused_computation.7.clone.1 | loop fusion | flops 25165824 | bytes 75530240 | tf_op jit(solution)/shard_map/while/body/eval_jaxpr/convert_element_type | solution.py:101
  677.3 12.8 fusion.129
  690.1 12.9 fusion.130
  704.1 13.9 convolution_add_fusion.2
  718.1 18.6 %fusion.127 = (f32[4,1024]{1,0:T(4,128)S(1)}, f32[4,1024,1024]{1,2,0:T(8,128)}) fusion(f32[4,1024,1024]{1,2,0:T(8,128)} %convolution_add_fusion.2), kind=kOutput, calls=%fused_computation.122.clone.1 | output fusion | flops 8389631 | bytes 33570816 | tf_op jit(solution)/shard_map/while/body/eval_jaxpr/sub | solution.py:88
  736.7 14.3 multiply_reduce_fusion.4
  751.0 23.3 %fusion.128 = (bf16[4,1024,1024]{1,2,0:T(8,128)(2,1)S(1)}, f32[4,1024,1024]{1,2,0:T(8,128)}) fusion(f32[4,1024,1024]{1,2,0:T(8,128)} %get-tuple-element.193, f32[4,1024]{1,0:T(4,128)S(1)} %get-tuple-element.194, f32[4,1024,1024]{1,2,0:T(8,128)} %get-tuple-element.191, f32[4,1024]{1,0:T(4,128)S(1)} %get-tuple-element.192, ...), kind=kLoop, calls=%fused_computation.7.clone.1 | loop fusion | flops 25165824 | bytes 75530240 | tf_op jit(solution)/shard_map/while/body/eval_jaxpr/convert_element_type | solution.py:101
  779.3 12.8 fusion.129
  792.2 12.9 fusion.130
  806.2 13.9 convolution_add_fusion.2
  820.1 18.6 %fusion.127 = (f32[4,1024]{1,0:T(4,128)S(1)}, f32[4,1024,1024]{1,2,0:T(8,128)}) fusion(f32[4,1024,1024]{1,2,0:T(8,128)} %convolution_add_fusion.2), kind=kOutput, calls=%fused_computation.122.clone.1 | output fusion | flops 8389631 | bytes 33570816 | tf_op jit(solution)/shard_map/while/body/eval_jaxpr/sub | solution.py:88
  838.7 14.3 multiply_reduce_fusion.4
  853.0 23.3 %fusion.128 = (bf16[4,1024,1024]{1,2,0:T(8,128)(2,1)S(1)}, f32[4,1024,1024]{1,2,0:T(8,128)}) fusion(f32[4,1024,1024]{1,2,0:T(8,128)} %get-tuple-element.193, f32[4,1024]{1,0:T(4,128)S(1)} %get-tuple-element.194, f32[4,1024,1024]{1,2,0:T(8,128)} %get-tuple-element.191, f32[4,1024]{1,0:T(4,128)S(1)} %get-tuple-element.192, ...), kind=kLoop, calls=%fused_computation.7.clone.1 | loop fusion | flops 25165824 | bytes 75530240 | tf_op jit(solution)/shard_map/while/body/eval_jaxpr/convert_element_type | solution.py:101
  881.4 12.8 fusion.129
  894.2 12.9 fusion.130
  908.2 13.9 convolution_add_fusion.2
  922.2 18.6 %fusion.127 = (f32[4,1024]{1,0:T(4,128)S(1)}, f32[4,1024,1024]{1,2,0:T(8,128)}) fusion(f32[4,1024,1024]{1,2,0:T(8,128)} %convolution_add_fusion.2), kind=kOutput, calls=%fused_computation.122.clone.1 | output fusion | flops 8389631 | bytes 33570816 | tf_op jit(solution)/shard_map/while/body/eval_jaxpr/sub | solution.py:88
  940.8 14.3 multiply_reduce_fusion.4
  955.1 23.3 %fusion.128 = (bf16[4,1024,1024]{1,2,0:T(8,128)(2,1)S(1)}, f32[4,1024,1024]{1,2,0:T(8,128)}) fusion(f32[4,1024,1024]{1,2,0:T(8,128)} %get-tuple-element.193, f32[4,1024]{1,0:T(4,128)S(1)} %get-tuple-element.194, f32[4,1024,1024]{1,2,0:T(8,128)} %get-tuple-element.191, f32[4,1024]{1,0:T(4,128)S(1)} %get-tuple-element.192, ...), kind=kLoop, calls=%fused_computation.7.clone.1 | loop fusion | flops 25165824 | bytes 75530240 | tf_op jit(solution)/shard_map/while/body/eval_jaxpr/convert_element_type | solution.py:101
  983.4 12.8 fusion.129
  996.3 12.9 fusion.130
  1010.3 20.2 %copy.73 = f32[4,1024,1024]{2,0,1:T(4,128)} copy(f32[4,1024,1024]{1,2,0:T(8,128)} %get-tuple-element.51) | data formatting | bytes 33554432 | tf_op jit(solution)/shard_map/while | solution.py:115
  1030.5 7.7 bitcast_convert_fusion
  1038.3 364.3 %all-reduce.2 = bf16[4,1024,1024]{2,0,1:T(4,128)(2,1)} all-reduce(f32[4,1024,1024]{2,0,1:T(4,128)} %copy.73), channel_id=3, replica_groups=mesh['seq'=16,'head'=2] {'seq'}, use_global_device_ids=true, to_apply=%region_12.13.clone | all-reduce | flops 4194304 | bytes 25165824
  1409.8 6.5 all-to-all-done.1
  1417.9 7.7 multiply_reduce_fusion.1
  1425.7 9.5 fusion.59
  1435.2 12.0 copy.76
  1451.2 5.5 multiply_convert_fusion
  (122 shorter events, 119.5 us)
Async XLA Ops:
  7.2 163.9 %copy-start = (bf16[256,256]{1,0:T(8,128)(2,1)S(1)}, bf16[256,256]{1,0:T(8,128)(2,1)}, u32[]{:S(2)}) copy-start(bf16[256,256]{1,0:T(8,128)(2,1)} %param.27) | copy-start | bytes 393220
  7.2 166.8 %all-gather.2.cloned.1.call-start = ((), (), s32[]{:S(2)}) async-start(), calls=%async_computation.3 | async-start | bytes 8912896 | tf_op jit(solution)/shard_map/all_gather | solution.py:46
  9.6 33.3 %copy-start.10 = (bf16[256,256]{1,0:T(8,128)(2,1)S(1)}, bf16[256,256]{1,0:T(8,128)(2,1)}, u32[]{:S(2)}) copy-start(bf16[256,256]{1,0:T(8,128)(2,1)} %param.25) | copy-start | bytes 393220
  11.3 31.7 %copy-start.11 = (bf16[256,256]{1,0:T(8,128)(2,1)S(1)}, bf16[256,256]{1,0:T(8,128)(2,1)}, u32[]{:S(2)}) copy-start(bf16[256,256]{1,0:T(8,128)(2,1)} %param.22) | copy-start | bytes 393220
  11.3 31.8 %copy-start.12 = (bf16[256,256]{1,0:T(8,128)(2,1)S(1)}, bf16[256,256]{1,0:T(8,128)(2,1)}, u32[]{:S(2)}) copy-start(bf16[256,256]{1,0:T(8,128)(2,1)} %param.24) | copy-start | bytes 393220
  13.0 30.2 %copy-start.13 = (bf16[256,256]{1,0:T(8,128)(2,1)S(1)}, bf16[256,256]{1,0:T(8,128)(2,1)}, u32[]{:S(2)}) copy-start(bf16[256,256]{1,0:T(8,128)(2,1)} %param.23) | copy-start | bytes 393220
  36.5 132.1 %all-to-all-start = ((bf16[16,8,64,256]{3,2,1,0:T(8,128)(2,1)}), bf16[16,8,64,256]{3,2,1,0:T(8,128)(2,1)}, u32[]{:S(2)}, u32[]{:S(2)}) async-start(bf16[16,8,64,256]{3,2,1,0:T(8,128)(2,1)} %bitcast_dynamic-update-slice_fusion), calls=%async_computation | async-start | bytes 8388608 | tf_op jit(solution)/shard_map/all_to_all | solution.py:66
  42.8 1404.4 %reduce-scatter.2.cloned.1.call-start = ((), (), s32[]{:S(2)}) async-start(), calls=%async_computation.4 | async-start | bytes 6291456 | tf_op jit(solution)/shard_map/reduce_scatter | solution.py:137
  43.3 12.2 copy-start.18
  43.3 12.2 copy-start.20
  56.8 8.4 copy-start.2
  56.8 10.5 copy-start.3
  56.8 10.5 copy-start.14
  56.8 10.5 copy-start.19
  65.3 22.8 %copy-start.8 = (f32[8,1024]{1,0:T(8,128)}, f32[8,1024]{1,0:T(8,128)S(1)}, u32[]{:S(2)}) copy-start(f32[8,1024]{1,0:T(8,128)S(1)} %add_rsqrt_fusion.1) | copy-start | bytes 98308
  67.4 16.8 %copy-start.4 = (f32[64,512]{1,0:T(8,128)}, f32[64,512]{1,0:T(8,128)S(1)}, u32[]{:S(2)}) copy-start(f32[64,512]{1,0:T(8,128)S(1)} %broadcast_multiply_fusion.2) | copy-start | bytes 393220
  1010.3 20.2 %copy-start.7 = (bf16[256,8,4,32]{0,3,2,1:T(8,128)(2,1)S(1)}, bf16[256,8,4,32]{0,3,2,1:T(8,128)(2,1)}, u32[]{:S(2)}) copy-start(bf16[256,8,4,32]{0,3,2,1:T(8,128)(2,1)} %copy.69) | copy-start | bytes 1572868
  1038.2 371.5 %copy-start.9 = (f32[8,1024]{1,0:T(8,128)S(1)}, f32[8,1024]{1,0:T(8,128)}, u32[]{:S(2)}) copy-start(f32[8,1024]{1,0:T(8,128)} %copy-done.8) | copy-start | bytes 98308
  1038.2 371.5 %copy-start.6 = (f32[64,512]{1,0:T(8,128)S(1)}, f32[64,512]{1,0:T(8,128)}, u32[]{:S(2)}) copy-start(f32[64,512]{1,0:T(8,128)} %fusion.60) | copy-start | bytes 393220
  1402.5 15.4 %copy-start.5 = (f32[64,512]{1,0:T(8,128)S(1)}, f32[64,512]{1,0:T(8,128)}, u32[]{:S(2)}) copy-start(f32[64,512]{1,0:T(8,128)} %copy-done.4) | copy-start | bytes 393220
  1402.5 15.4 %copy-start.16 = (f32[128]{0:T(128)S(1)}, f32[128]{0:T(128)}, u32[]{:S(2)}) copy-start(f32[128]{0:T(128)} %param.28) | copy-start | bytes 1540
  1402.5 15.4 %copy-start.17 = (bf16[128,8]{0,1:T(8,128)(2,1)S(1)}, bf16[128,8]{0,1:T(8,128)(2,1)}, u32[]{:S(2)}) copy-start(bf16[128,8]{0,1:T(8,128)(2,1)} %param.29) | copy-start | bytes 6148
  1406.2 10.1 all-to-all-start.1
  1435.2 12.0 copy-start.15
  1435.2 21.5 %copy-start.1 = (bf16[256,256]{1,0:T(8,128)(2,1)S(1)}, bf16[256,256]{1,0:T(8,128)(2,1)}, u32[]{:S(2)}) copy-start(bf16[256,256]{1,0:T(8,128)(2,1)} %param.27) | copy-start | bytes 393220
Sparse Core Ops, SparseCore 0:
  10.1 130.4 all-gather.1
  1038.4 54.3 reduce-scatter.1
